TPU v7x, 32 devices: a whole 2x2x4 slice. The times are simulated.
32 devices in a mesh: row: 4 (over x, core), tile: 8 (over z, y).
Axes of the slice: x: 2, y: 2, z: 4, core: 2. Of those that a mesh axis runs over, the one named last changes fastest.
Arguments:
- currents: bfloat16 [2, 4, 2, 128, 8192], P(None, None, None, ('row', 'tile')), may hold values from -6 to 6
- row_angles: int32 [2048], replicated, may hold values from 0 to 32767
- column_angles: int32 [2048], replicated, may hold values from 0 to 32767
- target: float32 [2, 2048, 2048], P(None, 'tile', 'row'), may hold values from 2 to 14
- weight: float32 [2, 2048, 2048], P(None, 'tile', 'row'), may hold values from 0.01 to 0.1
- tile_owner: int32 [8192, 1], P(('row', 'tile')), may hold values from 0 to 31; in each aligned block of 256 rows (0 to 255, 256 to 511, ...) at most 16 rows name the same one
- face_slot: int32 [8192], P(('row', 'tile')), may hold values from 0 to 255
Outputs:
- intensity: float32 [2, 2048, 2048], P(None, 'tile', 'row')
- faces: float32 [2, 4, 2, 8192, 128], P(None, None, None, ('row', 'tile'))
Inputs may be any that keep to these rules, and one draw needn't show every extreme that they name: `tile_owner`: among the 256 segments of one device no owner is named more than 16 times, a bound that some block reaches.
All inputs are finite; a program needn't handle non-finite values.
Results may differ from a plain program's by a relative error of at most 0.0085.
Values may be sent and summed in bfloat16 or wider, within the bound.
No kernel may reach another device: no remote copies, remote signals or barrier semaphores. Data moves between devices by JAX's collectives and lax.ppermute only.
A program may use at most 128 MiB of HBM per device.

v0:
```python
import math
import jax
import jax.numpy as jnp
from jax import lax
from jax.sharding import PartitionSpec as P

SEG = 128


def phase_pair(position, angles, modulus, scale):
    turns = position[:, None] * angles[None, :] % modulus
    angle = turns.astype(jnp.float32) * (2.0 * math.pi / modulus)
    return (jnp.cos(angle) * scale, jnp.sin(angle) * scale)


def spread_back(half):
    return jnp.stack([half[:, 0], half[:, 1], -half[:, 1], half[:, 0]], axis=1)


def polarize(fields):
    return jnp.stack([fields[:, 0] + fields[:, 3], fields[:, 1] - fields[:, 2]], axis=1)


def body(currents, row_angles, column_angles, target, weight, tile_owner, face_slot):
    row_count = lax.axis_size("row")
    tile_count = lax.axis_size("tile")
    devices = row_count * tile_count
    freq_count, comp_count, part_count, rows_dev, columns = currents.shape
    far_rows = row_angles.shape[0]
    far_cols = column_angles.shape[0]
    share_cols = far_cols // tile_count
    modulus = 4 * columns
    column_scale = 1.0 / math.sqrt(columns)
    row_scale = 1.0 / math.sqrt(rows_dev * devices)
    block_width = min(512, far_cols)
    block_count = far_cols // block_width
    channel_count = freq_count * comp_count
    column_index = jnp.arange(columns, dtype=jnp.int32)
    channels = currents.reshape(channel_count * part_count, rows_dev, columns)

    def column_block(offset):
        angles = lax.dynamic_slice_in_dim(column_angles, offset, block_width)
        cos_part, sin_part = phase_pair(column_index, angles, modulus, column_scale)
        return (cos_part.astype(jnp.bfloat16), sin_part.astype(jnp.bfloat16))

    def forward_step(state, offset):
        cos_part, sin_part = column_block(offset)
        table = jnp.stack([cos_part, sin_part], axis=1)
        products = jnp.einsum("qxy,ysv->qsvx", channels, table, preferred_element_type=jnp.float32)
        products = products.reshape(channel_count, 2, 2, block_width, rows_dev)
        real_part = products[:, 0, 0] + products[:, 1, 1]
        imag_part = products[:, 1, 0] - products[:, 0, 1]
        return (state, jnp.stack([real_part, imag_part], axis=1).astype(jnp.bfloat16))

    block_starts = jnp.arange(block_count, dtype=jnp.int32) * block_width
    _, column_pieces = lax.scan(forward_step, jnp.int32(0), block_starts)
    ordered_cols = jnp.moveaxis(column_pieces, 0, 2)
    plane_cols = ordered_cols.reshape(channel_count * part_count, tile_count, share_cols * rows_dev)
    received = lax.all_to_all(plane_cols, "tile", split_axis=1, concat_axis=1, tiled=True)
    received = received.reshape(channel_count, 2, tile_count, share_cols, rows_dev)
    here_row = lax.axis_index("row")
    group_pos = here_row * (tile_count * rows_dev) + jnp.arange(
        tile_count * rows_dev, dtype=jnp.int32
    )
    row_cos, row_sin = phase_pair(group_pos, row_angles, modulus, row_scale)
    row_cos = row_cos.astype(jnp.bfloat16).reshape(tile_count, rows_dev, far_rows)
    row_sin = row_sin.astype(jnp.bfloat16).reshape(tile_count, rows_dev, far_rows)
    table_real = jnp.stack([row_cos, row_sin])
    table_imag = jnp.stack([-row_sin, row_cos])
    field_re = jnp.einsum(
        "qrtvx,rtxu->qvu", received, table_real, preferred_element_type=jnp.float32
    )
    field_im = jnp.einsum(
        "qrtvx,rtxu->qvu", received, table_imag, preferred_element_type=jnp.float32
    )
    field_re = field_re.reshape(freq_count, comp_count, share_cols, far_rows)
    field_im = field_im.reshape(freq_count, comp_count, share_cols, far_rows)
    fields = jnp.stack([field_re, field_im], axis=2)
    own_fields = polarize(lax.psum_scatter(fields, "row", scatter_dimension=4, tiled=True))
    intensity = jnp.sum(own_fields * own_fields, axis=(1, 2))
    factor = 4.0 * weight * (intensity - target)
    far_grad = (factor[:, None, None] * own_fields).astype(jnp.bfloat16)
    portion = lax.all_gather(far_grad, "row", axis=4, tiled=True)
    extent = portion.shape[4]
    angles = row_angles
    piece_cos, piece_sin = phase_pair(group_pos, angles, modulus, row_scale)
    piece_cos = piece_cos.astype(jnp.bfloat16).reshape(tile_count, rows_dev, extent)
    piece_sin = piece_sin.astype(jnp.bfloat16).reshape(tile_count, rows_dev, extent)
    back_real = jnp.stack([piece_cos, -piece_sin])
    back_imag = jnp.stack([piece_sin, piece_cos])
    next_re = jnp.einsum(
        "fprvu,rtxu->fptvx", portion, back_real, preferred_element_type=jnp.float32
    )
    next_im = jnp.einsum(
        "fprvu,rtxu->fptvx", portion, back_imag, preferred_element_type=jnp.float32
    )
    back_re = next_re
    back_im = next_im
    plane_grad = jnp.stack([spread_back(back_re), spread_back(back_im)], axis=2).astype(
        jnp.bfloat16
    )
    plane_grad = plane_grad.reshape(channel_count * part_count, tile_count, share_cols * rows_dev)
    returned = lax.all_to_all(plane_grad, "tile", split_axis=1, concat_axis=1, tiled=True)
    returned = returned.reshape(channel_count, 2, far_cols, rows_dev)

    def adjoint_step(totals, offset):
        cos_part, sin_part = column_block(offset)
        grad_block = lax.dynamic_slice_in_dim(returned, offset, block_width, axis=2)
        with_cos = jnp.einsum(
            "qrvx,yv->qrxy", grad_block, cos_part, preferred_element_type=jnp.float32
        )
        with_sin = jnp.einsum(
            "qrvx,yv->qrxy", grad_block, sin_part, preferred_element_type=jnp.float32
        )
        next_re = totals[0] + with_cos[:, 0] - with_sin[:, 1]
        next_im = totals[1] + with_sin[:, 0] + with_cos[:, 1]
        return ((next_re, next_im), None)

    plane_zero = jnp.zeros((channel_count, rows_dev, columns), jnp.float32)
    (adjoint_re, adjoint_im), _ = lax.scan(adjoint_step, (plane_zero, plane_zero), block_starts)
    adjoint = jnp.stack([adjoint_re, adjoint_im], axis=1).astype(jnp.bfloat16)
    segments = adjoint.reshape(channel_count * part_count, rows_dev * columns // SEG, SEG)
    seg_count = segments.shape[1]
    capacity = max(2, 2 * seg_count // devices)
    owner_index = tile_owner[:, 0]
    matches = (owner_index[:, None] == jnp.arange(devices, dtype=jnp.int32)[None, :]).astype(
        jnp.int32
    )
    earlier = jnp.cumsum(matches, axis=0) - matches
    ranked = jnp.sum(earlier * matches, axis=1)
    position = owner_index * capacity + ranked
    outgoing = jnp.zeros((channel_count * part_count, devices * capacity, SEG), jnp.bfloat16)
    outgoing = outgoing.at[:, position].set(segments)
    labels = jnp.full((devices * capacity,), seg_count, jnp.int32).at[position].set(face_slot)
    arrived, slot_marks = (
        lax.all_to_all(
            outgoing.reshape(channel_count * part_count, devices, capacity, SEG),
            ("row", "tile"),
            split_axis=1,
            concat_axis=1,
            tiled=True,
        ),
        lax.all_to_all(
            labels.reshape(1, devices, capacity),
            ("row", "tile"),
            split_axis=1,
            concat_axis=1,
            tiled=True,
        ),
    )
    arrived = arrived.reshape(channel_count * part_count, devices * capacity, SEG).astype(
        jnp.float32
    )
    slot_marks = slot_marks.reshape(devices * capacity)
    faces = jnp.zeros((channel_count * part_count, seg_count, SEG), jnp.float32)
    faces = faces.at[:, slot_marks].add(arrived, mode="drop")
    return (intensity, faces.reshape(freq_count, comp_count, part_count, seg_count, SEG))


def solution(mesh):
    in_specs = (
        P(None, None, None, ("row", "tile"), None),
        P(),
        P(),
        P(None, "tile", "row"),
        P(None, "tile", "row"),
        P(("row", "tile"), None),
        P(("row", "tile")),
    )
    out_specs = (P(None, "tile", "row"), P(None, None, None, ("row", "tile"), None))
    return jax.shard_map(body, mesh=mesh, in_specs=in_specs, out_specs=out_specs, check_vma=False)
```

profile of v0, /device:TPU:0, one launch (start us, length us, event | category | flops | bytes accessed | tf_op | source)
XLA Modules:
  0.0 1409.9 jit_solution(18253644668635062543)
XLA Ops:
  9.0 300.6 %while.28 = (s32[]{:T(128)}, bf16[4,8,2,512,4]{3,1,4,2,0:T(8,128)(2,1)S(1)}, s32[4]{0:T(128)S(1)}, s32[2048]{0:T(1024)}, bf16[16,4,8192]{2,0,1:T(8,128)(2,1)S(1)}, /*index=5*/s32[]{:T(128)}, s32[]{:T(128)}, s32[]{:T(128)}) while((s32[]{:T(128)}, bf16[4,8,2,512,4]{3,1,4,2,0:T(8,128)(2,1)S(1)}, s32[4]{0:T(128)S(1)}, s32[2048]{0:T(1024)}, ...), condition=%wide.region_1.2_spmd.clone, body=%wide.region_0.1_spmd.clone.sunk | while | flops 1182990336 | bytes 36378764 | solution.py:56
  12.3 67.9 %multiply_convert_fusion.8 = (bf16[8192,1,512]{2,0,1:T(8,128)(2,1)S(1)}, bf16[8192,1,512]{2,0,1:T(8,128)(2,1)S(1)}) fusion(s32[512]{0:T(512)S(1)} %dynamic_slice.53), kind=kLoop, calls=%fused_computation.16.clone.1 | loop fusion | flops 75497472 | bytes 16779264 | tf_op jit(solution)/shard_map/while/body/eval_jaxpr/convert_element_type | solution.py:44
  80.3 3.4 fusion.115
  87.5 67.9 %multiply_convert_fusion.8 = (bf16[8192,1,512]{2,0,1:T(8,128)(2,1)S(1)}, bf16[8192,1,512]{2,0,1:T(8,128)(2,1)S(1)}) fusion(s32[512]{0:T(512)S(1)} %dynamic_slice.53), kind=kLoop, calls=%fused_computation.16.clone.1 | loop fusion | flops 75497472 | bytes 16779264 | tf_op jit(solution)/shard_map/while/body/eval_jaxpr/convert_element_type | solution.py:44
  155.4 3.4 fusion.115
  162.6 67.9 %multiply_convert_fusion.8 = (bf16[8192,1,512]{2,0,1:T(8,128)(2,1)S(1)}, bf16[8192,1,512]{2,0,1:T(8,128)(2,1)S(1)}) fusion(s32[512]{0:T(512)S(1)} %dynamic_slice.53), kind=kLoop, calls=%fused_computation.16.clone.1 | loop fusion | flops 75497472 | bytes 16779264 | tf_op jit(solution)/shard_map/while/body/eval_jaxpr/convert_element_type | solution.py:44
  230.6 3.4 fusion.115
  237.7 67.9 %multiply_convert_fusion.8 = (bf16[8192,1,512]{2,0,1:T(8,128)(2,1)S(1)}, bf16[8192,1,512]{2,0,1:T(8,128)(2,1)S(1)}) fusion(s32[512]{0:T(512)S(1)} %dynamic_slice.53), kind=kLoop, calls=%fused_computation.16.clone.1 | loop fusion | flops 75497472 | bytes 16779264 | tf_op jit(solution)/shard_map/while/body/eval_jaxpr/convert_element_type | solution.py:44
  305.7 3.4 fusion.115
  309.6 6.0 copy.43
  315.6 17.0 %reshape.427 = bf16[16,8,1024]{2,1,0:T(8,128)(2,1)S(1)} reshape(bf16[8,2,4,512,4]{4,3,2,1,0:T(8,128)(2,1)} %copy.43) | data formatting | bytes 524288 | tf_op jit(solution)/shard_map/reshape | solution.py:58
  333.5 7.3 all-to-all-start
  343.3 6.3 all-to-all-done
  349.7 3.1 copy.45
  352.8 5.2 copy.46
  358.0 2.4 convolution_bitcast_fusion.1
  360.4 2.4 convolution_bitcast_fusion
  362.8 11.7 pad_maximum_fusion
  375.0 233.4 %reduce-scatter.2.cloned.1.call-done = f32[2,4,2,256,512]{4,3,1,0,2:T(8,128)} async-done(((f32[2,4,2,256,2048]{4,3,1,0,2:T(8,128)}), f32[2,4,2,256,512]{4,3,1,0,2:T(8,128)}) %reduce-scatter.2.cloned.1.call-update) | async-done | bytes 8388624 | tf_op jit(solution)/shard_map/reduce_scatter | solution.py:79
  608.5 4.5 slice_add_fusion
  617.0 58.4 %all-gather.2.cloned.1.call-done = bf16[2,2,2,256,2048]{4,3,1,0,2:T(8,128)(2,1)} async-done(((bf16[2,2,2,256,512]{4,3,1,0,2:T(8,128)(2,1)}), bf16[2,2,2,256,2048]{4,3,1,0,2:T(8,128)(2,1)}) %all-gather.2.cloned.1.call-update) | async-done | bytes 8388624 | tf_op jit(solution)/shard_map/all_gather | solution.py:83
  675.4 6.0 fusion.87
  681.5 2.5 fusion.88
  684.2 4.5 copy.53
  688.7 4.4 copy.54
  693.2 5.5 all-to-all-start.2
  701.9 6.1 all-to-all-done.2
  708.0 3.1 all-to-all-start.1
  711.3 19.0 %reshape.433 = bf16[8,2,2048,4]{3,2,1,0:T(8,128)(2,1)} reshape(bf16[16,8,1024]{2,1,0:T(8,128)(2,1)S(1)} %copy.55) | data formatting | bytes 524288 | tf_op jit(solution)/shard_map/reshape | solution.py:104
  730.3 7.1 copy.56
  737.4 532.7 %while.29 = (s32[]{:T(128)}, f32[8,4,8192]{2,0,1:T(8,128)S(1)}, f32[8,4,8192]{2,0,1:T(8,128)}, s32[4]{0:T(128)S(1)}, bf16[8,2,2048,4]{2,0,3,1:T(8,128)(2,1)S(1)}...) while((s32[]{:T(128)}, f32[8,4,8192]{2,0,1:T(8,128)S(1)}, f32[8,4,8192]{2,0,1:T(8,128)}, ...), condition=%wide.region_9.10_spmd.clone, body=%wide.region_8.9_spmd.clone.sunk | while | flops 1209532416 | bytes 12722337 | solution.py:120
  740.9 62.6 %fusion.123 = f32[8,2,4,8192]{3,0,2,1:T(8,128)S(1)} fusion(s32[512]{0:T(512)S(1)} %dynamic_slice.57, bf16[8,2,2048,4]{2,0,3,1:T(8,128)(2,1)S(1)} %get-tuple-element.405, s32[]{:T(128)S(6)} %select_n.142), kind=kOutput, calls=%fused_computation.44.clone.3 | convolution fusion | flops 603979776 | bytes 2164740 | tf_op jit(solution)/shard_map/while/body/eval_jaxpr/qrvx,yv->qrxy/dot_general | solution.py:112
  803.5 63.4 %fusion.122 = f32[8,2,4,8192]{3,0,2,1:T(8,128)} fusion(s32[512]{0:T(512)S(1)} %dynamic_slice.57, bf16[8,2,2048,4]{2,0,3,1:T(8,128)(2,1)S(1)} %get-tuple-element.405, s32[]{:T(128)S(6)} %select_n.142), kind=kOutput, calls=%fused_computation.42.clone.3 | convolution fusion | flops 603979776 | bytes 2164740 | tf_op jit(solution)/shard_map/while/body/eval_jaxpr/qrvx,yv->qrxy/dot_general | solution.py:109
  866.9 3.5 fusion.124
  873.8 62.6 %fusion.123 = f32[8,2,4,8192]{3,0,2,1:T(8,128)S(1)} fusion(s32[512]{0:T(512)S(1)} %dynamic_slice.57, bf16[8,2,2048,4]{2,0,3,1:T(8,128)(2,1)S(1)} %get-tuple-element.405, s32[]{:T(128)S(6)} %select_n.142), kind=kOutput, calls=%fused_computation.44.clone.3 | convolution fusion | flops 603979776 | bytes 2164740 | tf_op jit(solution)/shard_map/while/body/eval_jaxpr/qrvx,yv->qrxy/dot_general | solution.py:112
  936.3 63.4 %fusion.122 = f32[8,2,4,8192]{3,0,2,1:T(8,128)} fusion(s32[512]{0:T(512)S(1)} %dynamic_slice.57, bf16[8,2,2048,4]{2,0,3,1:T(8,128)(2,1)S(1)} %get-tuple-element.405, s32[]{:T(128)S(6)} %select_n.142), kind=kOutput, calls=%fused_computation.42.clone.3 | convolution fusion | flops 603979776 | bytes 2164740 | tf_op jit(solution)/shard_map/while/body/eval_jaxpr/qrvx,yv->qrxy/dot_general | solution.py:109
  999.8 3.8 fusion.124
  1006.9 62.6 %fusion.123 = f32[8,2,4,8192]{3,0,2,1:T(8,128)S(1)} fusion(s32[512]{0:T(512)S(1)} %dynamic_slice.57, bf16[8,2,2048,4]{2,0,3,1:T(8,128)(2,1)S(1)} %get-tuple-element.405, s32[]{:T(128)S(6)} %select_n.142), kind=kOutput, calls=%fused_computation.44.clone.3 | convolution fusion | flops 603979776 | bytes 2164740 | tf_op jit(solution)/shard_map/while/body/eval_jaxpr/qrvx,yv->qrxy/dot_general | solution.py:112
  1069.5 63.4 %fusion.122 = f32[8,2,4,8192]{3,0,2,1:T(8,128)} fusion(s32[512]{0:T(512)S(1)} %dynamic_slice.57, bf16[8,2,2048,4]{2,0,3,1:T(8,128)(2,1)S(1)} %get-tuple-element.405, s32[]{:T(128)S(6)} %select_n.142), kind=kOutput, calls=%fused_computation.42.clone.3 | convolution fusion | flops 603979776 | bytes 2164740 | tf_op jit(solution)/shard_map/while/body/eval_jaxpr/qrvx,yv->qrxy/dot_general | solution.py:109
  1132.9 3.8 fusion.124
  1140.1 62.6 %fusion.123 = f32[8,2,4,8192]{3,0,2,1:T(8,128)S(1)} fusion(s32[512]{0:T(512)S(1)} %dynamic_slice.57, bf16[8,2,2048,4]{2,0,3,1:T(8,128)(2,1)S(1)} %get-tuple-element.405, s32[]{:T(128)S(6)} %select_n.142), kind=kOutput, calls=%fused_computation.44.clone.3 | convolution fusion | flops 603979776 | bytes 2164740 | tf_op jit(solution)/shard_map/while/body/eval_jaxpr/qrvx,yv->qrxy/dot_general | solution.py:112
  1202.6 63.4 %fusion.122 = f32[8,2,4,8192]{3,0,2,1:T(8,128)} fusion(s32[512]{0:T(512)S(1)} %dynamic_slice.57, bf16[8,2,2048,4]{2,0,3,1:T(8,128)(2,1)S(1)} %get-tuple-element.405, s32[]{:T(128)S(6)} %select_n.142), kind=kOutput, calls=%fused_computation.42.clone.3 | convolution fusion | flops 603979776 | bytes 2164740 | tf_op jit(solution)/shard_map/while/body/eval_jaxpr/qrvx,yv->qrxy/dot_general | solution.py:109
  1266.1 3.8 fusion.124
  1275.8 25.5 %scatter_fusion = bf16[16,512,128]{2,0,1:T(8,128)(2,1)} fusion(bf16[16,512,128]{2,0,1:T(8,128)(2,1)} %broadcast_in_dim.14, s32[256]{0:T(256)S(1)} %bitcast.193, bf16[256,16,128]{2,1,0:T(8,128)(2,1)S(1)} %copy.58), kind=kCustom, calls=%fused_computation.1 | custom fusion | bytes 3146752 | tf_op jit(solution)/shard_map/scatter | solution.py:133
  1301.3 5.8 all-to-all-start.3
  1309.2 48.0 %all-to-all-done.3 = bf16[16,32,16,128]{3,0,2,1:T(8,128)(2,1)S(1)} async-done(((bf16[16,32,16,128]{3,0,2,1:T(8,128)(2,1)}), bf16[16,32,16,128]{3,0,2,1:T(8,128)(2,1)S(1)}, u32[]{:S(2)}, u32[]{:S(2)}) %all-to-all-start.3) | async-done | bytes 2097184 | tf_op jit(solution)/shard_map/all_to_all | solution.py:136
  1357.2 2.4 convert_bitcast_fusion
  1359.8 41.0 %scatter_fusion.1 = f32[16,256,128]{2,0,1:T(8,128)S(1)} fusion(f32[16,256,128]{2,0,1:T(8,128)S(1)} %broadcast_in_dim.13, s32[512]{0:T(512)S(1)} %bitcast.191, f32[512,16,128]{2,1,0:T(8,128)} %convert_bitcast_fusion), kind=kCustom, calls=%fused_computation.2 | custom fusion | flops 1048576 | bytes 12584960 | tf_op jit(solution)/shard_map/scatter-add | solution.py:156
  (98 shorter events, 35.5 us)
Async XLA Ops:
  309.6 31.5 %copy-start.3 = (s32[2048]{0:T(1024)S(1)}, s32[2048]{0:T(1024)}, u32[]{:S(2)}) copy-start(s32[2048]{0:T(1024)} %param.12) | copy-start | bytes 24580
  333.5 16.2 %all-to-all-start = ((bf16[16,8,1024]{2,0,1:T(8,128)(2,1)}), bf16[16,8,1024]{2,0,1:T(8,128)(2,1)S(1)}, u32[]{:S(2)}, u32[]{:S(2)}) async-start(bf16[16,8,1024]{2,0,1:T(8,128)(2,1)} %copy.44), calls=%async_computation | async-start | bytes 524288 | tf_op jit(solution)/shard_map/all_to_all | solution.py:59
  340.8 267.7 %reduce-scatter.2.cloned.1.call-start = ((), (), s32[]{:S(2)}) async-start(), calls=%async_computation.5 | async-start | bytes 41943040 | tf_op jit(solution)/shard_map/reduce_scatter | solution.py:79
  374.5 240.0 %copy-start.1 = (f32[2,256,512]{2,1,0:T(8,128)S(1)}, f32[2,256,512]{2,1,0:T(8,128)}, u32[]{:S(2)}) copy-start(f32[2,256,512]{2,1,0:T(8,128)} %param.14) | copy-start | bytes 3145732
  374.5 240.0 %copy-start.2 = (f32[2,256,512]{2,1,0:T(8,128)S(1)}, f32[2,256,512]{2,1,0:T(8,128)}, u32[]{:S(2)}) copy-start(f32[2,256,512]{2,1,0:T(8,128)} %param.15) | copy-start | bytes 3145732
  374.5 300.9 %all-gather.2.cloned.1.call-start = ((), (), s32[]{:S(2)}) async-start(), calls=%async_computation.6 | async-start | bytes 10485760 | tf_op jit(solution)/shard_map/all_gather | solution.py:83
  613.5 1.0 copy-start
  675.4 6.1 slice-start
  675.4 6.1 slice-start.1
  684.0 14.6 %copy-start.4 = (s32[256,1]{0,1:T(1,128)S(1)}, s32[256,1]{0,1:T(1,128)}, u32[]{:S(2)}) copy-start(s32[256,1]{0,1:T(1,128)} %param.16) | copy-start | bytes 3076
  693.2 14.9 %all-to-all-start.2 = ((bf16[16,8,1024]{2,0,1:T(8,128)(2,1)}), bf16[16,8,1024]{2,0,1:T(8,128)(2,1)S(1)}, u32[]{:S(2)}, u32[]{:S(2)}) async-start(bf16[16,8,1024]{2,0,1:T(8,128)(2,1)} %copy.54), calls=%async_computation.3 | async-start | bytes 524288 | tf_op jit(solution)/shard_map/all_to_all | solution.py:103
  699.6 8.4 copy-start.5
  708.0 593.3 %all-to-all-start.1 = ((s32[1,32,16]{2,0,1:T(1,128)}), s32[1,32,16]{2,0,1:T(1,128)}, u32[]{:S(2)}, u32[]{:S(2)}) async-start(s32[1,32,16]{2,0,1:T(1,128)} %bitcast.20), calls=%async_computation.2 | async-start | bytes 32768 | tf_op jit(solution)/shard_map/all_to_all | solution.py:143
  1270.1 5.7 copy-start.6
  1301.3 55.9 %all-to-all-start.3 = ((bf16[16,32,16,128]{3,0,2,1:T(8,128)(2,1)}), bf16[16,32,16,128]{3,0,2,1:T(8,128)(2,1)S(1)}, u32[]{:S(2)}, u32[]{:S(2)}) async-start(bf16[16,32,16,128]{3,0,2,1:T(8,128)(2,1)} %bitcast.40), calls=%async_computation.4 | async-start | bytes 4194304 | tf_op jit(solution)/shard_map/all_to_all | solution.py:136
Sparse Core Ops, SparseCore 0:
  374.6 233.7 reduce-scatter.1
  617.1 58.2 all-gather.1
where the time goes:
time: 1420 us; the launch traced here: 1410 us
  matrix products  531 us (37%)
  other arithmetic  356 us (25%)
  waiting for transfers between devices  352 us (25%)
  local copies, waits for them, and re-layouts  118 us (8%)
  starting transfers between devices  22.4 us (2%)
  loops' own time  16.2 us (1%)
  between operations  14.8 us (1%)
    convert_element_type x4, other arithmetic, column_block(): return (cos_part.astype(jnp.bfloat16), sin_part.astype(jnp.bfloat16))  272 us
    dot_general x4, matrix products, adjoint_step(): jnp.einsum('qrvx,yv->qrxy', grad_block, cos_part, preferred_element_type=...  254 us
    dot_general x4, matrix products, adjoint_step(): jnp.einsum('qrvx,yv->qrxy', grad_block, sin_part, preferred_element_type=...  250 us
    reduce_scatter x1, waiting for transfers between devices, body(): lax.psum_scatter(fields, 'row', scatter_dimension=4, tiled=True)  233 us
    all_gather x1, waiting for transfers between devices, body(): portion = lax.all_gather(far_grad, 'row', axis=4, tiled=True)  58.4 us
    all_to_all x1, waiting for transfers between devices, body(): lax.all_to_all(outgoing.reshape(channel_count * part_count, devices, capa...  48 us
    scatter-add x1, other arithmetic, body(): faces = faces.at[:, slot_marks].add(arrived, mode='drop')  41 us
  transfers between devices with their start and end apart: 6, of which 5 were waited for; matrix products, arithmetic and copies ran while one was open for 42% of the time, Pallas kernels for 0%

commit v1 on v0

--- a/solution.py
+++ b/solution.py
@@ -5,6 +5,16 @@
 from jax.sharding import PartitionSpec as P
 
 SEG = 128
+
+
+def view_words(piece_in, bus_axis, k_dim, array_axis=1):
+    left_arr = jnp.concatenate(
+        jax.lax.all_to_all(
+            jnp.stack(jnp.split(piece_in, jax.lax.axis_size(bus_axis), k_dim), 0), bus_axis, 0, 0
+        ),
+        array_axis,
+    )
+    return left_arr
 
 
 def phase_pair(position, angles, modulus, scale):
@@ -133,12 +143,8 @@
     outgoing = outgoing.at[:, position].set(segments)
     labels = jnp.full((devices * capacity,), seg_count, jnp.int32).at[position].set(face_slot)
     arrived, slot_marks = (
-        lax.all_to_all(
-            outgoing.reshape(channel_count * part_count, devices, capacity, SEG),
-            ("row", "tile"),
-            split_axis=1,
-            concat_axis=1,
-            tiled=True,
+        view_words(
+            outgoing.reshape(channel_count * part_count, devices, capacity, SEG), ("row", "tile"), 1
         ),
         lax.all_to_all(
             labels.reshape(1, devices, capacity),

time: 1420 us -> 1410 us (level)
    unnamed x20 -> x51, local copies, waits for them, and re-layouts: 10.1 us -> 29.7 us
    scatter x1, local copies, waits for them, and re-layouts: 25.5 us -> 7.06 us  [body(): outgoing = outgoing.at[:, position].set(segments)]
where the time goes in v1:
time: 1410 us
  matrix products  531 us (38%)
  other arithmetic  356 us (25%)
  waiting for transfers between devices  353 us (25%)
  local copies, waits for them, and re-layouts  112 us (8%)
  starting transfers between devices  22.6 us (2%)
  loops' own time  16.2 us (1%)
  between operations  14.8 us (1%)
    convert_element_type x4, other arithmetic, column_block(): return (cos_part.astype(jnp.bfloat16), sin_part.astype(jnp.bfloat16))  272 us
    dot_general x4, matrix products, adjoint_step(): jnp.einsum('qrvx,yv->qrxy', grad_block, cos_part, preferred_element_type=...  254 us
    dot_general x4, matrix products, adjoint_step(): jnp.einsum('qrvx,yv->qrxy', grad_block, sin_part, preferred_element_type=...  250 us
    reduce_scatter x1, waiting for transfers between devices, body(): lax.psum_scatter(fields, 'row', scatter_dimension=4, tiled=True)  233 us
    all_gather x1, waiting for transfers between devices, body(): portion = lax.all_gather(far_grad, 'row', axis=4, tiled=True)  58.4 us
    all_to_all x1, waiting for transfers between devices, view_words(): jax.lax.all_to_all(jnp.stack(jnp.split(piece_in, jax.lax.axis_size(bus_ax...  48.2 us
    scatter-add x1, other arithmetic, body(): faces = faces.at[:, slot_marks].add(arrived, mode='drop')  41 us
    unnamed x51, local copies, waits for them, and re-layouts  29.7 us
  transfers between devices with their start and end apart: 6, of which 5 were waited for; matrix products, arithmetic and copies ran while one was open for 42% of the time, Pallas kernels for 0%

profile of v1, /device:TPU:0, one launch (start us, length us, event | category | flops | bytes accessed | tf_op | source)
XLA Modules:
  0.0 1405.1 jit_solution(13566668627208986877)
XLA Ops:
  9.0 297.9 %while.28 = (s32[]{:T(128)}, bf16[4,8,2,512,4]{3,1,4,2,0:T(8,128)(2,1)S(1)}, s32[4]{0:T(128)S(1)}, s32[2048]{0:T(1024)S(1)}, bf16[16,4,8192]{2,0,1:T(8,128)(2,1)S(1)}, /*index=5*/s32[]{:T(128)}, s32[]{:T(128)}, s32[]{:T(128)}) while((s32[]{:T(128)}, bf16[4,8,2,512,4]{3,1,4,2,0:T(8,128)(2,1)S(1)}, s32[4]{0:T(128)S(1)}, ...), condition=%wide.region_1.2_spmd.clone, body=%wide.region_0.1_spmd.clone.sunk | while | flops 1182990336 | bytes 36378764 | solution.py:66
  11.6 68.0 %multiply_convert_fusion.8 = (bf16[8192,1,512]{2,0,1:T(8,128)(2,1)S(1)}, bf16[8192,1,512]{2,0,1:T(8,128)(2,1)S(1)}) fusion(s32[512]{0:T(512)S(1)} %dynamic_slice.53), kind=kLoop, calls=%fused_computation.16.clone.1 | loop fusion | flops 75497472 | bytes 16779264 | tf_op jit(solution)/shard_map/while/body/eval_jaxpr/convert_element_type | solution.py:54
  79.6 3.4 fusion.115
  86.1 68.0 %multiply_convert_fusion.8 = (bf16[8192,1,512]{2,0,1:T(8,128)(2,1)S(1)}, bf16[8192,1,512]{2,0,1:T(8,128)(2,1)S(1)}) fusion(s32[512]{0:T(512)S(1)} %dynamic_slice.53), kind=kLoop, calls=%fused_computation.16.clone.1 | loop fusion | flops 75497472 | bytes 16779264 | tf_op jit(solution)/shard_map/while/body/eval_jaxpr/convert_element_type | solution.py:54
  154.1 3.4 fusion.115
  160.6 68.0 %multiply_convert_fusion.8 = (bf16[8192,1,512]{2,0,1:T(8,128)(2,1)S(1)}, bf16[8192,1,512]{2,0,1:T(8,128)(2,1)S(1)}) fusion(s32[512]{0:T(512)S(1)} %dynamic_slice.53), kind=kLoop, calls=%fused_computation.16.clone.1 | loop fusion | flops 75497472 | bytes 16779264 | tf_op jit(solution)/shard_map/while/body/eval_jaxpr/convert_element_type | solution.py:54
  228.6 3.4 fusion.115
  235.1 68.0 %multiply_convert_fusion.8 = (bf16[8192,1,512]{2,0,1:T(8,128)(2,1)S(1)}, bf16[8192,1,512]{2,0,1:T(8,128)(2,1)S(1)}) fusion(s32[512]{0:T(512)S(1)} %dynamic_slice.53), kind=kLoop, calls=%fused_computation.16.clone.1 | loop fusion | flops 75497472 | bytes 16779264 | tf_op jit(solution)/shard_map/while/body/eval_jaxpr/convert_element_type | solution.py:54
  303.1 3.4 fusion.115
  306.9 6.0 copy.43
  312.9 17.0 %reshape.427 = bf16[16,8,1024]{2,1,0:T(8,128)(2,1)S(1)} reshape(bf16[8,2,4,512,4]{4,3,2,1,0:T(8,128)(2,1)} %copy.43) | data formatting | bytes 524288 | tf_op jit(solution)/shard_map/reshape | solution.py:68
  330.8 7.3 all-to-all-start
  340.7 6.3 all-to-all-done
  347.0 3.1 copy.45
  350.1 5.2 copy.46
  355.4 2.4 convolution_bitcast_fusion.1
  357.8 2.4 convolution_bitcast_fusion
  360.1 11.6 pad_maximum_fusion
  372.3 233.4 %reduce-scatter.2.cloned.1.call-done = f32[2,4,2,256,512]{4,3,1,0,2:T(8,128)} async-done(((f32[2,4,2,256,2048]{4,3,1,0,2:T(8,128)}), f32[2,4,2,256,512]{4,3,1,0,2:T(8,128)}) %reduce-scatter.2.cloned.1.call-update) | async-done | bytes 8388624 | tf_op jit(solution)/shard_map/reduce_scatter | solution.py:89
  605.8 4.5 slice_add_fusion
  614.3 58.4 %all-gather.2.cloned.1.call-done = bf16[2,2,2,256,2048]{4,3,1,0,2:T(8,128)(2,1)} async-done(((bf16[2,2,2,256,512]{4,3,1,0,2:T(8,128)(2,1)}), bf16[2,2,2,256,2048]{4,3,1,0,2:T(8,128)(2,1)}) %all-gather.2.cloned.1.call-update) | async-done | bytes 8388624 | tf_op jit(solution)/shard_map/all_gather | solution.py:93
  672.8 6.0 fusion.87
  678.8 2.5 fusion.88
  681.5 4.5 copy.53
  686.0 4.5 copy.54
  690.4 5.5 all-to-all-start.2
  699.2 6.1 all-to-all-done.2
  705.3 3.3 all-to-all-start.1
  708.7 19.0 %reshape.433 = bf16[8,2,2048,4]{3,2,1,0:T(8,128)(2,1)} reshape(bf16[16,8,1024]{2,1,0:T(8,128)(2,1)S(1)} %copy.55) | data formatting | bytes 524288 | tf_op jit(solution)/shard_map/reshape | solution.py:114
  727.7 7.1 copy.56
  734.8 529.9 %while.29 = (s32[]{:T(128)}, f32[8,4,8192]{2,0,1:T(8,128)S(1)}, f32[8,4,8192]{2,0,1:T(8,128)}, s32[4]{0:T(128)S(1)}, bf16[8,2,2048,4]{2,0,3,1:T(8,128)(2,1)S(1)}...) while((s32[]{:T(128)}, f32[8,4,8192]{2,0,1:T(8,128)S(1)}, f32[8,4,8192]{2,0,1:T(8,128)}, ...), condition=%wide.region_9.10_spmd.clone, body=%wide.region_8.9_spmd.clone.sunk | while | flops 1209532416 | bytes 12722337 | solution.py:130
  737.6 62.6 %fusion.123 = f32[8,2,4,8192]{3,0,2,1:T(8,128)S(1)} fusion(s32[512]{0:T(512)S(1)} %dynamic_slice.57, bf16[8,2,2048,4]{2,0,3,1:T(8,128)(2,1)S(1)} %get-tuple-element.405, s32[]{:T(128)S(6)} %select_n.142), kind=kOutput, calls=%fused_computation.44.clone.3 | convolution fusion | flops 603979776 | bytes 2164740 | tf_op jit(solution)/shard_map/while/body/eval_jaxpr/qrvx,yv->qrxy/dot_general | solution.py:122
  800.2 63.4 %fusion.122 = f32[8,2,4,8192]{3,0,2,1:T(8,128)} fusion(s32[512]{0:T(512)S(1)} %dynamic_slice.57, bf16[8,2,2048,4]{2,0,3,1:T(8,128)(2,1)S(1)} %get-tuple-element.405, s32[]{:T(128)S(6)} %select_n.142), kind=kOutput, calls=%fused_computation.42.clone.3 | convolution fusion | flops 603979776 | bytes 2164740 | tf_op jit(solution)/shard_map/while/body/eval_jaxpr/qrvx,yv->qrxy/dot_general | solution.py:119
  863.6 3.5 fusion.124
  869.8 62.6 %fusion.123 = f32[8,2,4,8192]{3,0,2,1:T(8,128)S(1)} fusion(s32[512]{0:T(512)S(1)} %dynamic_slice.57, bf16[8,2,2048,4]{2,0,3,1:T(8,128)(2,1)S(1)} %get-tuple-element.405, s32[]{:T(128)S(6)} %select_n.142), kind=kOutput, calls=%fused_computation.44.clone.3 | convolution fusion | flops 603979776 | bytes 2164740 | tf_op jit(solution)/shard_map/while/body/eval_jaxpr/qrvx,yv->qrxy/dot_general | solution.py:122
  932.3 63.4 %fusion.122 = f32[8,2,4,8192]{3,0,2,1:T(8,128)} fusion(s32[512]{0:T(512)S(1)} %dynamic_slice.57, bf16[8,2,2048,4]{2,0,3,1:T(8,128)(2,1)S(1)} %get-tuple-element.405, s32[]{:T(128)S(6)} %select_n.142), kind=kOutput, calls=%fused_computation.42.clone.3 | convolution fusion | flops 603979776 | bytes 2164740 | tf_op jit(solution)/shard_map/while/body/eval_jaxpr/qrvx,yv->qrxy/dot_general | solution.py:119
  995.8 3.8 fusion.124
  1002.2 62.6 %fusion.123 = f32[8,2,4,8192]{3,0,2,1:T(8,128)S(1)} fusion(s32[512]{0:T(512)S(1)} %dynamic_slice.57, bf16[8,2,2048,4]{2,0,3,1:T(8,128)(2,1)S(1)} %get-tuple-element.405, s32[]{:T(128)S(6)} %select_n.142), kind=kOutput, calls=%fused_computation.44.clone.3 | convolution fusion | flops 603979776 | bytes 2164740 | tf_op jit(solution)/shard_map/while/body/eval_jaxpr/qrvx,yv->qrxy/dot_general | solution.py:122
  1064.8 63.4 %fusion.122 = f32[8,2,4,8192]{3,0,2,1:T(8,128)} fusion(s32[512]{0:T(512)S(1)} %dynamic_slice.57, bf16[8,2,2048,4]{2,0,3,1:T(8,128)(2,1)S(1)} %get-tuple-element.405, s32[]{:T(128)S(6)} %select_n.142), kind=kOutput, calls=%fused_computation.42.clone.3 | convolution fusion | flops 603979776 | bytes 2164740 | tf_op jit(solution)/shard_map/while/body/eval_jaxpr/qrvx,yv->qrxy/dot_general | solution.py:119
  1128.2 3.8 fusion.124
  1134.7 62.6 %fusion.123 = f32[8,2,4,8192]{3,0,2,1:T(8,128)S(1)} fusion(s32[512]{0:T(512)S(1)} %dynamic_slice.57, bf16[8,2,2048,4]{2,0,3,1:T(8,128)(2,1)S(1)} %get-tuple-element.405, s32[]{:T(128)S(6)} %select_n.142), kind=kOutput, calls=%fused_computation.44.clone.3 | convolution fusion | flops 603979776 | bytes 2164740 | tf_op jit(solution)/shard_map/while/body/eval_jaxpr/qrvx,yv->qrxy/dot_general | solution.py:122
  1197.3 63.4 %fusion.122 = f32[8,2,4,8192]{3,0,2,1:T(8,128)} fusion(s32[512]{0:T(512)S(1)} %dynamic_slice.57, bf16[8,2,2048,4]{2,0,3,1:T(8,128)(2,1)S(1)} %get-tuple-element.405, s32[]{:T(128)S(6)} %select_n.142), kind=kOutput, calls=%fused_computation.42.clone.3 | convolution fusion | flops 603979776 | bytes 2164740 | tf_op jit(solution)/shard_map/while/body/eval_jaxpr/qrvx,yv->qrxy/dot_general | solution.py:119
  1260.7 3.8 fusion.124
  1269.1 7.1 scatter_fusion
  1296.5 5.8 all-to-all-start.3
  1304.2 48.2 %all-to-all-done.3 = bf16[32,16,1,16,128]{4,1,3,2,0:T(8,128)(2,1)S(1)} async-done(((bf16[32,16,1,16,128]{4,1,3,2,0:T(8,128)(2,1)}), bf16[32,16,1,16,128]{4,1,3,2,0:T(8,128)(2,1)S(1)}, u32[]{:S(2)}, u32[]{:S(2)}) %all-to-all-start.3) | async-done | bytes 2097184 | tf_op jit(solution)/shard_map/all_to_all | solution.py:12
  1352.3 2.5 convert_element_type.163
  1354.9 41.0 %scatter_fusion.1 = f32[16,256,128]{2,0,1:T(8,128)S(1)} fusion(f32[16,256,128]{2,0,1:T(8,128)S(1)} %broadcast_in_dim.13, s32[512]{0:T(512)S(1)} %bitcast.352, f32[512,16,128]{2,1,0:T(8,128)} %bitcast.310), kind=kCustom, calls=%fused_computation.2 | custom fusion | flops 1048576 | bytes 12584960 | tf_op jit(solution)/shard_map/scatter-add | solution.py:162
  (129 shorter events, 48.8 us)
Async XLA Ops:
  7.2 1.8 copy-start.3
  312.9 25.5 %copy-start.4 = (s32[2048]{0:T(1024)S(1)}, s32[2048]{0:T(1024)}, u32[]{:S(2)}) copy-start(s32[2048]{0:T(1024)} %param.12) | copy-start | bytes 24580
  330.8 16.2 %all-to-all-start = ((bf16[16,8,1024]{2,0,1:T(8,128)(2,1)}), bf16[16,8,1024]{2,0,1:T(8,128)(2,1)S(1)}, u32[]{:S(2)}, u32[]{:S(2)}) async-start(bf16[16,8,1024]{2,0,1:T(8,128)(2,1)} %copy.44), calls=%async_computation | async-start | bytes 524288 | tf_op jit(solution)/shard_map/all_to_all | solution.py:69
  338.1 267.7 %reduce-scatter.2.cloned.1.call-start = ((), (), s32[]{:S(2)}) async-start(), calls=%async_computation.5 | async-start | bytes 41943040 | tf_op jit(solution)/shard_map/reduce_scatter | solution.py:89
  371.8 301.0 %all-gather.2.cloned.1.call-start = ((), (), s32[]{:S(2)}) async-start(), calls=%async_computation.6 | async-start | bytes 10485760 | tf_op jit(solution)/shard_map/all_gather | solution.py:93
  610.2 1.6 copy-start.1
  610.2 1.6 copy-start.2
  610.9 1.0 copy-start
  672.8 6.1 copy-start.8
  686.0 10.0 copy-start.5
  690.4 14.9 %all-to-all-start.2 = ((bf16[16,8,1024]{2,0,1:T(8,128)(2,1)}), bf16[16,8,1024]{2,0,1:T(8,128)(2,1)S(1)}, u32[]{:S(2)}, u32[]{:S(2)}) async-start(bf16[16,8,1024]{2,0,1:T(8,128)(2,1)} %copy.54), calls=%async_computation.3 | async-start | bytes 524288 | tf_op jit(solution)/shard_map/all_to_all | solution.py:113
  696.9 8.4 copy-start.6
  705.3 591.2 %all-to-all-start.1 = ((s32[1,32,16]{2,0,1:T(1,128)}), s32[1,32,16]{2,0,1:T(1,128)}, u32[]{:S(2)}, u32[]{:S(2)}) async-start(s32[1,32,16]{2,0,1:T(1,128)} %bitcast.20), calls=%async_computation.2 | async-start | bytes 32768 | tf_op jit(solution)/shard_map/all_to_all | solution.py:149
  1268.1 1.0 copy-start.7
  1296.5 55.9 %all-to-all-start.3 = ((bf16[32,16,1,16,128]{4,1,3,2,0:T(8,128)(2,1)}), bf16[32,16,1,16,128]{4,1,3,2,0:T(8,128)(2,1)S(1)}, u32[]{:S(2)}, u32[]{:S(2)}) async-start(bf16[32,16,1,16,128]{4,1,3,2,0:T(8,128)(2,1)} %constant_dynamic-update-slice_fusion), calls=%async_computation.4 | async-start | bytes 4194304 | tf_op jit(solution)/shard_map/all_to_all | solution.py:12
Sparse Core Ops, SparseCore 0:
  371.9 233.7 reduce-scatter.1
  614.4 58.2 all-gather.1
